TPU v7x, 32 devices: a whole 2x2x4 slice. The times are simulated.
32 devices in a mesh: order: 4 (over z), band: 4 (over x, core), chan: 2 (over y).
Axes of the slice: x: 2, y: 2, z: 4, core: 2. Of those that a mesh axis runs over, the one named last changes fastest.
Arguments:
- coef_grad: bfloat16 [2, 368, 2, 384, 361], P('chan', ('order', 'band')), may hold values from -6 to 6
- coef_saved: bfloat16 [2, 368, 2, 73, 361], P('chan', ('order', 'band')), may hold values from -0.016601562 to 0.016601562
- lift_weight: bfloat16 [384, 73], replicated, may hold values from -0.3125 to 0.3125
- legendre: bfloat16 [368, 361, 16], P(('order', 'band')), may hold values from -0.3125 to 0.3125
- order_of_slot: int32 [368], replicated, may hold values from 0 to 367, as said below
- trunc_degree: int32 [2], P('chan'), may hold values from 271 to 360
Outputs:
- grid_grad: bfloat16 [2, 73, 16, 1440], P('chan', None, ('order', 'band'))
- weight_grad: float32 [384, 73], P(('order', 'band'))
Inputs may be any that keep to these rules, and one draw needn't show every extreme that they name: order_of_slot holds each of 0 to 367 once; in the g-th block of 23 slots, slot s holds s * 16 + k_g for even s and s * 16 + 15 - k_g for odd s, where k is a permutation of 0 to 15.
All inputs are finite; a program needn't handle non-finite values.
Results may differ from a plain program's by a relative error of at most 0.0062.
Values may be sent and summed in bfloat16 or wider, within the bound.
No kernel may reach another device: no remote copies, remote signals or barrier semaphores. Data moves between devices by JAX's collectives and lax.ppermute only.
A program may use at most 64 MiB of HBM per device.

v0:
```python
import math
import jax
import jax.numpy as jnp
from jax import lax
from jax.sharding import PartitionSpec as P

LON = 1440


def local(coef_grad, coef_saved, lift_weight, legendre, order_of_slot, trunc_degree):
    samp_dev = coef_grad.shape[0]
    slot_dev = coef_grad.shape[1]
    degrees = coef_grad.shape[4]
    chan_in = coef_saved.shape[3]
    pair_width = 2 * chan_in
    groups = lax.axis_size(("order", "band"))
    slot_count = order_of_slot.shape[0]
    first_slot = lax.axis_index(("order", "band")) * slot_dev
    local_orders = lax.dynamic_slice_in_dim(order_of_slot, first_slot, slot_dev)
    degree_ids = jnp.arange(degrees, dtype=jnp.int32)
    live_mask = (degree_ids[None, None, :] >= local_orders[None, :, None]) & (
        degree_ids[None, None, :] <= trunc_degree[:, None, None]
    )
    kept_grad = jnp.where(live_mask[:, :, None, None, :], coef_grad, jnp.zeros((), coef_grad.dtype))
    lifted = jnp.einsum(
        "pqrel,ec->pqrcl", kept_grad, lift_weight, preferred_element_type=jnp.float32
    ).astype(jnp.bfloat16)
    lifted = lifted.reshape(samp_dev, slot_dev, pair_width, degrees)
    own_rows = lax.psum_scatter(
        jnp.einsum("pqrel,pqrcl->ec", kept_grad, coef_saved, preferred_element_type=jnp.float32),
        ("order", "band"),
        scatter_dimension=0,
        tiled=True,
    )
    weight_grad = lax.psum(own_rows, "chan")
    spectral = jnp.einsum(
        "qlt,pqjl->pqtj", legendre, lifted, preferred_element_type=jnp.float32
    ).astype(jnp.bfloat16)
    lat_dev = spectral.shape[2] // groups
    lon_ids = jnp.arange(LON, dtype=jnp.int32)
    angles = (order_of_slot[:, None] * lon_ids[None, :] % LON).astype(jnp.float32) * (
        2.0 * math.pi / LON
    )
    angle_table = jnp.stack([jnp.cos(angles), -jnp.sin(angles)], axis=1).astype(jnp.bfloat16)
    synth_scale = 1.0 / math.sqrt(LON)
    received = lax.all_to_all(spectral, ("order", "band"), split_axis=2, concat_axis=1, tiled=True)
    item_count = received.shape[0]
    split_parts = received.reshape(item_count, slot_count, lat_dev, 2, chan_in)
    synth_field = jnp.einsum(
        "pqtrc,qrn->pctn", split_parts, angle_table, preferred_element_type=jnp.float32
    )
    grid_grad = (synth_field * synth_scale).astype(jnp.bfloat16)
    return (grid_grad, weight_grad)


def solution(mesh):
    return jax.shard_map(
        local,
        mesh=mesh,
        in_specs=(
            P("chan", ("order", "band"), None, None, None),
            P("chan", ("order", "band"), None, None, None),
            P(),
            P(("order", "band"), None, None),
            P(),
            P("chan"),
        ),
        out_specs=(P("chan", None, ("order", "band"), None), P(("order", "band"), None)),
        check_vma=False,
    )
```

profile of v0, /device:TPU:0, one launch (start us, length us, event | category | flops | bytes accessed | tf_op | source)
XLA Modules:
  0.0 113.4 jit_solution(15885522489254012622)
XLA Ops:
  7.2 0.0 copy-start
  7.2 0.0 reduce-scatter.4.cloned.1.call-start
  8.0 0.8 dynamic_slice.3
  8.8 0.1 fusion.34
  8.9 19.3 %fusion = bf16[23,2,384,361]{2,1,3,0:T(2,128)(2,1)S(1)} fusion(bf16[1,23,2,384,361]{3,2,4,1,0:T(2,128)(2,1)} %param.6, pred[23,361]{1,0:T(8,128)(4,1)S(1)} %fusion.34), kind=kLoop, calls=%fused_computation.1 | loop fusion | flops 6376704 | bytes 25515120 | tf_op jit(solution)/shard_map/reshape.9
  28.2 0.0 copy-done
  28.2 0.0 copy-start.1
  28.2 4.6 %copy-done.1 = bf16[23,2,384,361]{2,1,3,0:T(2,128)(2,1)} copy-done((bf16[23,2,384,361]{2,1,3,0:T(2,128)(2,1)}, bf16[23,2,384,361]{2,1,3,0:T(2,128)(2,1)S(1)}, u32[]{:S(2)}) %copy-start.1) | copy-done | bytes 12753432
  32.8 4.7 %fusion.24 = f32[384,73]{1,0:T(8,128)} fusion(bf16[23,2,73,361]{3,1,2,0:T(2,128)(2,1)S(1)} %bitcast.44, bf16[23,2,384,361]{2,1,3,0:T(2,128)(2,1)S(1)} %fusion), kind=kOutput, calls=%fused_computation.27 | convolution fusion | flops 930998784 | bytes 15290012 | tf_op jit(solution)/shard_map/pqrel,pqrcl->ec/dot_general | solution.py:30
  37.4 0.0 reduce-scatter.4.cloned.1.call-update
  37.5 0.0 copy-done.4
  37.5 9.0 %convert_bitcast_fusion = bf16[1,23,2,73,361]{4,3,2,1,0:T(8,128)(2,1)S(1)} fusion(bf16[23,2,384,361]{2,1,3,0:T(2,128)(2,1)} %copy-done.1, bf16[384,73]{0,1:T(8,128)(2,1)S(1)} %copy-done.4), kind=kOutput, calls=%fused_computation.8 | convolution fusion | flops 932211008 | bytes 15233948 | tf_op jit(solution)/shard_map/pqrel,ec->pqrcl/dot_general | solution.py:25
  46.5 1.0 copy.19
  47.5 0.0 copy-start.2
  47.6 0.0 copy-done.3
  47.6 1.0 fusion.29
  48.6 0.8 copy.21
  49.4 7.4 %all-to-all-start = ((bf16[1,23,16,146]{3,1,0,2:T(8,128)(2,1)}), bf16[1,23,16,146]{3,1,0,2:T(8,128)(2,1)S(1)}, u32[]{:S(2)}, u32[]{:S(2)}) async-start(bf16[1,23,16,146]{3,1,0,2:T(8,128)(2,1)} %copy.21), calls=%async_computation | async-start | bytes 393216 | tf_op jit(solution)/shard_map/all_to_all | solution.py:46
  56.7 10.4 %cosine_convert_fusion = (bf16[368,1,1440]{0,2,1:T(8,128)(2,1)}, bf16[368,1,1440]{0,2,1:T(8,128)(2,1)}) fusion(s32[368]{0:T(512)S(1)} %copy-done.2), kind=kLoop, calls=%fused_computation.21 | loop fusion | flops 6359040 | bytes 2121152 | tf_op jit(solution)/shard_map/convert
  67.2 26.8 %reduce-scatter.4.cloned.1.call-done = f32[24,73]{1,0:T(8,128)} async-done(((f32[384,73]{1,0:T(8,128)}), f32[24,73]{1,0:T(8,128)}) %reduce-scatter.4.cloned.1.call-update) | async-done | bytes 7024
  94.0 9.3 %psum.7 = f32[24,73]{1,0:T(8,128)} all-reduce(f32[24,73]{1,0:T(8,128)} %reduce-scatter.4.cloned.1.call-done), channel_id=1, replica_groups=mesh['order'=4,'band'=4,'chan'=2] {'chan'}, use_global_device_ids=true, to_apply=%region_1.2 | all-reduce | flops 1752 | bytes 14016 | tf_op jit(solution)/shard_map/psum | solution.py:35
  103.3 0.0 all-to-all-done
  103.3 0.2 reshape.167
  103.5 3.1 %fusion.10 = bf16[1,73,1,1440]{3,1,2,0:T(8,128)(2,1)} fusion(bf16[368,1,1440]{0,2,1:T(8,128)(2,1)} %get-tuple-element.3, bf16[368,1,1440]{0,2,1:T(8,128)(2,1)} %get-tuple-element.2, bf16[368,2,73]{2,1,0:T(2,128)(2,1)S(1)} %reshape.167), kind=kOutput, calls=%fused_computation.14 | convolution fusion | flops 156006720 | bytes 2437376 | tf_op jit(solution)/shard_map/pqtrc,qrn->pctn/dot_general | solution.py:49
  (4 shorter events, 0.0 us)
Async XLA Ops:
  7.2 21.0 %copy-start = (bf16[1,23,2,73,361]{4,2,3,1,0:T(2,128)(2,1)S(1)}, bf16[1,23,2,73,361]{4,2,3,1,0:T(2,128)(2,1)}, u32[]{:S(2)}) copy-start(bf16[1,23,2,73,361]{4,2,3,1,0:T(2,128)(2,1)} %param.7) | copy-start | bytes 7273432
  7.2 86.8 %reduce-scatter.4.cloned.1.call-start = ((), (), s32[]{:S(2)}) async-start(), calls=%async_computation.2 | async-start | bytes 208896
  28.2 4.6 %copy-start.1 = (bf16[23,2,384,361]{2,1,3,0:T(2,128)(2,1)}, bf16[23,2,384,361]{2,1,3,0:T(2,128)(2,1)S(1)}, u32[]{:S(2)}) copy-start(bf16[23,2,384,361]{2,1,3,0:T(2,128)(2,1)S(1)} %fusion) | copy-start | bytes 38260228
  32.8 4.7 %copy-start.4 = (bf16[384,73]{0,1:T(8,128)(2,1)S(1)}, bf16[384,73]{0,1:T(8,128)(2,1)}, u32[]{:S(2)}) copy-start(bf16[384,73]{0,1:T(8,128)(2,1)} %param.8) | copy-start | bytes 168196
  46.5 1.0 copy-start.3
  47.5 9.2 %copy-start.2 = (s32[368]{0:T(512)S(1)}, s32[368]{0:T(512)}, u32[]{:S(2)}) copy-start(s32[368]{0:T(512)} %param.10) | copy-start | bytes 4420
  49.4 54.0 %all-to-all-start = ((bf16[1,23,16,146]{3,1,0,2:T(8,128)(2,1)}), bf16[1,23,16,146]{3,1,0,2:T(8,128)(2,1)S(1)}, u32[]{:S(2)}, u32[]{:S(2)}) async-start(bf16[1,23,16,146]{3,1,0,2:T(8,128)(2,1)} %copy.21), calls=%async_computation | async-start | bytes 393216 | tf_op jit(solution)/shard_map/all_to_all | solution.py:46
Sparse Core Ops, SparseCore 0:
  37.6 56.3 reduce-scatter.3
where the time goes:
time: 114 us; the launch traced here: 113 us
  other arithmetic  29.8 us (26%)
  waiting for transfers between devices  26.8 us (24%)
  matrix products  17.8 us (16%)
  between operations  14.9 us (13%)
  blocking collectives  9.35 us (8%)
  starting transfers between devices  7.4 us (6%)
  local copies, waits for them, and re-layouts  7.26 us (6%)
    another operation x2, other arithmetic  29.7 us
    unnamed x2, waiting for transfers between devices  26.8 us
    psum x1, blocking collectives, local(): weight_grad = lax.psum(own_rows, 'chan')  9.35 us
    dot_general x1, matrix products, local(): jnp.einsum('pqrel,ec->pqrcl', kept_grad, lift_weight, preferred_element_t...  9.05 us
    all_to_all x1, starting transfers between devices, local(): lax.all_to_all(spectral, ('order', 'band'), split_axis=2, concat_axis=1,...  7.36 us
    dot_general x1, matrix products, local(): jnp.einsum('pqrel,pqrcl->ec', kept_grad, coef_saved, preferred_element_ty...  4.66 us
    unnamed x10, local copies, waits for them, and re-layouts  4.58 us
    dot_general x1, matrix products, local(): jnp.einsum('pqtrc,qrn->pctn', split_parts, angle_table, preferred_element...  3.07 us
  transfers between devices with their start and end apart: 2, of which 1 were waited for; matrix products, arithmetic and copies ran while one was open for 20% of the time, Pallas kernels for 0%

commit v1 on v0

--- a/solution.py
+++ b/solution.py
@@ -43,7 +43,23 @@
     )
     angle_table = jnp.stack([jnp.cos(angles), -jnp.sin(angles)], axis=1).astype(jnp.bfloat16)
     synth_scale = 1.0 / math.sqrt(LON)
-    received = lax.all_to_all(spectral, ("order", "band"), split_axis=2, concat_axis=1, tiled=True)
+    r2, latest = (lax.axis_size(("order", "band")), lax.axis_index(("order", "band")))
+    arr_out = spectral.shape[2] // r2
+    a_now = list(spectral.shape)
+    a_now[2] = arr_out
+    vec_out = a_now[1]
+    a_now[1] = vec_out * r2
+    received = jnp.zeros(a_now, spectral.dtype)
+    for k0 in [*range(r2)]:
+        e_next = lax.dynamic_slice_in_dim(spectral, (latest ^ k0) * arr_out, arr_out, axis=2)
+        if k0:
+            parts_seen = []
+            for ix in [*range(r2)]:
+                parts_seen.append((ix, ix ^ k0))
+            e_next = lax.ppermute(e_next, axis_name=("order", "band"), perm=parts_seen)
+        received = lax.dynamic_update_slice_in_dim(
+            received, e_next, (latest ^ k0) * vec_out, axis=1
+        )
     item_count = received.shape[0]
     split_parts = received.reshape(item_count, slot_count, lat_dev, 2, chan_in)
     synth_field = jnp.einsum(

time: 114 us -> 131 us (1.15)
  starting transfers between devices: 7.4 us -> 22.3 us
  waiting for transfers between devices: 26.8 us -> 20.8 us
  local copies, waits for them, and re-layouts: 7.26 us -> 13.1 us
  matrix products: 17.8 us -> 19.6 us
    ppermute x0 -> x15, starting transfers between devices: none -> 22.2 us  [local(): e_next = lax.ppermute(e_next, axis_name=('order', 'band'), perm=parts_seen)]
    all_to_all x1 -> x0, starting transfers between devices: 7.36 us -> none  [local(): lax.all_to_all(spectral, ('order', 'band'), split_axis=2, concat_axis=1,...]
    dynamic_update_slice x0 -> x16, local copies, waits for them, and re-layouts: none -> 7.18 us  [local(): lax.dynamic_update_slice_in_dim(received, e_next, (latest ^ k0) * vec_out...]
    unnamed x2, waiting for transfers between devices: 26.8 us -> 20.7 us
    dot_general x1, matrix products: 9.05 us -> 4.5 us  [local(): jnp.einsum('pqrel,ec->pqrcl', kept_grad, lift_weight, preferred_element_t...]
    dot_general x1, matrix products: 4.66 us -> 9.18 us  [local(): jnp.einsum('pqrel,pqrcl->ec', kept_grad, coef_saved, preferred_element_ty...]
    unnamed x10 -> x25, local copies, waits for them, and re-layouts: 4.58 us -> 0.15 us
    ppermute x0 -> x15, local copies, waits for them, and re-layouts: none -> 1.89 us  [local(): e_next = lax.ppermute(e_next, axis_name=('order', 'band'), perm=parts_seen)]
  transfers between devices with their start and end apart: 2 -> 16, of which waited for: 1 -> 1; matrix products, arithmetic and copies ran while one was open for 20% -> 25% of each run, Pallas kernels for 0% -> 0%
where the time goes in v1:
time: 131 us; the launch traced here: 130 us
  other arithmetic  29.8 us (23%)
  starting transfers between devices  22.3 us (17%)
  waiting for transfers between devices  20.8 us (16%)
  matrix products  19.6 us (15%)
  between operations  15.3 us (12%)
  local copies, waits for them, and re-layouts  13.1 us (10%)
  blocking collectives  9.36 us (7%)
    another operation x2, other arithmetic  29.8 us
    ppermute x15, starting transfers between devices, local(): e_next = lax.ppermute(e_next, axis_name=('order', 'band'), perm=parts_seen)  22.2 us
    unnamed x2, waiting for transfers between devices  20.7 us
    psum x1, blocking collectives, local(): weight_grad = lax.psum(own_rows, 'chan')  9.36 us
    dot_general x1, matrix products, local(): jnp.einsum('pqrel,pqrcl->ec', kept_grad, coef_saved, preferred_element_ty...  9.18 us
    dynamic_update_slice x16, local copies, waits for them, and re-layouts, local(): lax.dynamic_update_slice_in_dim(received, e_next, (latest ^ k0) * vec_out...  7.18 us
    dot_general x1, matrix products, local(): jnp.einsum('pqrel,ec->pqrcl', kept_grad, lift_weight, preferred_element_t...  4.5 us
    dot_general x1, matrix products, local(): jnp.einsum('pqtrc,qrn->pctn', split_parts, angle_table, preferred_element...  3.1 us
  transfers between devices with their start and end apart: 16, of which 1 were waited for; matrix products, arithmetic and copies ran while one was open for 25% of the time, Pallas kernels for 0%

profile of v1, /device:TPU:0, one launch (start us, length us, event | category | flops | bytes accessed | tf_op | source)
XLA Modules:
  0.0 130.2 jit_solution(4156554771931021326)
XLA Ops:
  8.1 0.8 dynamic_slice.51
  9.0 19.3 %fusion = bf16[23,2,384,361]{2,1,3,0:T(2,128)(2,1)S(1)} fusion(bf16[1,23,2,384,361]{3,2,4,1,0:T(2,128)(2,1)} %param.6, pred[23,361]{1,0:T(8,128)(4,1)S(1)} %fusion.30), kind=kLoop, calls=%fused_computation.1 | loop fusion | flops 6376704 | bytes 25515120 | tf_op jit(solution)/shard_map/reshape.9
  28.3 4.5 %convert_bitcast_fusion = bf16[1,23,2,73,361]{4,3,2,1,0:T(8,128)(2,1)S(1)} fusion(bf16[23,2,384,361]{2,1,3,0:T(2,128)(2,1)S(1)} %fusion, bf16[384,73]{0,1:T(8,128)(2,1)S(1)} %copy-done.4), kind=kOutput, calls=%fused_computation.8 | convolution fusion | flops 932211008 | bytes 15233948 | tf_op jit(solution)/shard_map/pqrel,ec->pqrcl/dot_general | solution.py:25
  32.9 2.5 %copy.33 = bf16[1,23,2,73,361]{4,1,3,2,0:T(8,128)(2,1)} copy(bf16[1,23,2,73,361]{4,3,2,1,0:T(8,128)(2,1)S(1)} %convert_bitcast_fusion) | data formatting | bytes 4848952 | tf_op jit(solution)/shard_map/convert_element_type | solution.py:27
  35.4 2.8 %fusion.21 = bf16[23,146,16]{1,2,0:T(8,128)(2,1)S(1)} fusion(bf16[23,361,16]{1,2,0:T(8,128)(2,1)S(1)} %copy-done.3, bf16[23,146,361]{2,0,1:T(8,128)(2,1)} %bitcast.85), kind=kOutput, calls=%fused_computation.26 | convolution fusion | flops 38845344 | bytes 2797628 | tf_op jit(solution)/shard_map/qlt,pqjl->pqtj/dot_general | solution.py:36
  38.6 0.5 collective-permute-start
  39.2 2.6 %collective-permute-start.1 = (bf16[1,23,1,146]{3,1,2,0:T(8,128)(2,1)S(1)}, bf16[1,23,1,146]{3,1,2,0:T(8,128)(2,1)S(1)}, u32[]{:S(2)}, u32[]{:S(2)}) collective-permute-start(bf16[1,23,1,146]{3,1,2,0:T(8,128)(2,1)S(1)} %bitcast.100), channel_id=1, source_target_pairs={{0,4},{2,6},{4,0},{6,2},{8,12},{10,14},{12,8},{14,10},{16,20},{18,... | collective-permute-start | bytes 20156 | tf_op jit(solution)/shard_map/ppermute | solution.py:59
  41.9 1.8 %collective-permute-start.3 = (bf16[1,23,1,146]{3,1,2,0:T(8,128)(2,1)S(1)}, bf16[1,23,1,146]{3,1,2,0:T(8,128)(2,1)S(1)}, u32[]{:S(2)}, u32[]{:S(2)}) collective-permute-start(bf16[1,23,1,146]{3,1,2,0:T(8,128)(2,1)S(1)} %bitcast.98), channel_id=1, source_target_pairs={{0,8},{2,10},{4,12},{6,14},{8,0},{10,2},{12,4},{14,6},{16,24},{18,... | collective-permute-start | bytes 20156 | tf_op jit(solution)/shard_map/ppermute | solution.py:59
  43.7 2.7 %collective-permute-start.5 = (bf16[1,23,1,146]{3,1,2,0:T(8,128)(2,1)S(1)}, bf16[1,23,1,146]{3,1,2,0:T(8,128)(2,1)S(1)}, u32[]{:S(2)}, u32[]{:S(2)}) collective-permute-start(bf16[1,23,1,146]{3,1,2,0:T(8,128)(2,1)S(1)} %bitcast.96), channel_id=1, source_target_pairs={{0,12},{2,14},{4,8},{6,10},{8,4},{10,6},{12,0},{14,2},{16,28},{18,... | collective-permute-start | bytes 20156 | tf_op jit(solution)/shard_map/ppermute | solution.py:59
  46.5 2.6 %collective-permute-start.7 = (bf16[1,23,1,146]{3,1,2,0:T(8,128)(2,1)S(1)}, bf16[1,23,1,146]{3,1,2,0:T(8,128)(2,1)S(1)}, u32[]{:S(2)}, u32[]{:S(2)}) collective-permute-start(bf16[1,23,1,146]{3,1,2,0:T(8,128)(2,1)S(1)} %bitcast.94), channel_id=1, source_target_pairs={{0,16},{2,18},{4,20},{6,22},{8,24},{10,26},{12,28},{14,30},{16,0},... | collective-permute-start | bytes 20156 | tf_op jit(solution)/shard_map/ppermute | solution.py:59
  49.2 3.5 %collective-permute-start.9 = (bf16[1,23,1,146]{3,1,2,0:T(8,128)(2,1)S(1)}, bf16[1,23,1,146]{3,1,2,0:T(8,128)(2,1)S(1)}, u32[]{:S(2)}, u32[]{:S(2)}) collective-permute-start(bf16[1,23,1,146]{3,1,2,0:T(8,128)(2,1)S(1)} %bitcast.92), channel_id=1, source_target_pairs={{0,20},{2,22},{4,16},{6,18},{8,28},{10,30},{12,24},{14,26},{16,4},... | collective-permute-start | bytes 20156 | tf_op jit(solution)/shard_map/ppermute | solution.py:59
  52.7 9.2 %fusion.24 = f32[384,73]{1,0:T(8,128)} fusion(bf16[23,2,73,361]{3,1,2,0:T(2,128)(2,1)S(1)} %bitcast.84, bf16[23,2,384,361]{2,1,3,0:T(2,128)(2,1)} %copy-done.1), kind=kOutput, calls=%fused_computation.27 | convolution fusion | flops 930998784 | bytes 15290012 | tf_op jit(solution)/shard_map/pqrel,pqrcl->ec/dot_general | solution.py:30
  62.1 3.6 %collective-permute-start.11 = (bf16[1,23,1,146]{3,1,2,0:T(8,128)(2,1)S(1)}, bf16[1,23,1,146]{3,1,2,0:T(8,128)(2,1)S(1)}, u32[]{:S(2)}, u32[]{:S(2)}) collective-permute-start(bf16[1,23,1,146]{3,1,2,0:T(8,128)(2,1)S(1)} %bitcast.90), channel_id=1, source_target_pairs={{0,24},{2,26},{4,28},{6,30},{8,16},{10,18},{12,20},{14,22},{16,8},... | collective-permute-start | bytes 20156 | tf_op jit(solution)/shard_map/ppermute | solution.py:59
  65.8 4.4 %collective-permute-start.13 = (bf16[1,23,1,146]{3,1,2,0:T(8,128)(2,1)S(1)}, bf16[1,23,1,146]{3,1,2,0:T(8,128)(2,1)S(1)}, u32[]{:S(2)}, u32[]{:S(2)}) collective-permute-start(bf16[1,23,1,146]{3,1,2,0:T(8,128)(2,1)S(1)} %bitcast.88), channel_id=1, source_target_pairs={{0,28},{2,30},{4,24},{6,26},{8,20},{10,22},{12,16},{14,18},{16,12}... | collective-permute-start | bytes 20156 | tf_op jit(solution)/shard_map/ppermute | solution.py:59
  70.3 10.4 %cosine_convert_fusion = (bf16[368,1,1440]{0,2,1:T(8,128)(2,1)}, bf16[368,1,1440]{0,2,1:T(8,128)(2,1)}) fusion(s32[368]{0:T(512)S(1)} %copy-done.2), kind=kLoop, calls=%fused_computation.21 | loop fusion | flops 6359040 | bytes 2121152 | tf_op jit(solution)/shard_map/convert
  81.3 0.5 dynamic_update_slice.49
  81.9 0.6 dynamic_update_slice.50
  82.7 0.5 dynamic_update_slice.51
  83.3 0.5 dynamic_update_slice.52
  83.9 0.5 dynamic_update_slice.53
  86.8 0.5 dynamic_update_slice.58
  90.2 3.1 %fusion.10 = bf16[1,73,1,1440]{3,1,2,0:T(8,128)(2,1)} fusion(bf16[368,2,73]{0,2,1:T(8,128)(2,1)S(1)} %reshape.214, bf16[368,1,1440]{0,2,1:T(8,128)(2,1)} %get-tuple-element.19, bf16[368,1,1440]{0,2,1:T(8,128)(2,1)} %get-tuple-element.18), kind=kOutput, calls=%fused_computation.14 | convolution fusion | flops 156006720 | bytes 2437376 | tf_op jit(solution)/shard_map/pqtrc,qrn->pctn/dot_general | solution.py:65
  93.3 20.7 %reduce-scatter.4.cloned.1.call-done = f32[24,73]{1,0:T(8,128)} async-done(((f32[384,73]{1,0:T(8,128)}), f32[24,73]{1,0:T(8,128)}) %reduce-scatter.4.cloned.1.call-update) | async-done | bytes 7024
  114.0 9.4 %psum.7 = f32[24,73]{1,0:T(8,128)} all-reduce(f32[24,73]{1,0:T(8,128)} %reduce-scatter.4.cloned.1.call-done), channel_id=1, replica_groups=mesh['order'=4,'band'=4,'chan'=2] {'chan'}, use_global_device_ids=true, to_apply=%region_1.2 | all-reduce | flops 1752 | bytes 14016 | tf_op jit(solution)/shard_map/psum | solution.py:35
  (80 shorter events, 7.7 us)
Async XLA Ops:
  7.2 45.5 %copy-start = (bf16[1,23,2,73,361]{4,2,3,1,0:T(2,128)(2,1)S(1)}, bf16[1,23,2,73,361]{4,2,3,1,0:T(2,128)(2,1)}, u32[]{:S(2)}) copy-start(bf16[1,23,2,73,361]{4,2,3,1,0:T(2,128)(2,1)} %param.7) | copy-start | bytes 7273432
  7.2 106.9 %reduce-scatter.4.cloned.1.call-start = ((), (), s32[]{:S(2)}) async-start(), calls=%async_computation.1 | async-start | bytes 208896
  8.9 19.3 %copy-start.4 = (bf16[384,73]{0,1:T(8,128)(2,1)S(1)}, bf16[384,73]{0,1:T(8,128)(2,1)}, u32[]{:S(2)}) copy-start(bf16[384,73]{0,1:T(8,128)(2,1)} %param.8) | copy-start | bytes 168196
  28.3 4.6 %copy-start.1 = (bf16[23,2,384,361]{2,1,3,0:T(2,128)(2,1)}, bf16[23,2,384,361]{2,1,3,0:T(2,128)(2,1)S(1)}, u32[]{:S(2)}) copy-start(bf16[23,2,384,361]{2,1,3,0:T(2,128)(2,1)S(1)} %fusion) | copy-start | bytes 38260228
  32.9 2.5 %copy-start.3 = (bf16[23,361,16]{1,2,0:T(8,128)(2,1)S(1)}, bf16[23,361,16]{1,2,0:T(8,128)(2,1)}, u32[]{:S(2)}) copy-start(bf16[23,361,16]{1,2,0:T(8,128)(2,1)} %param.9) | copy-start | bytes 797092
  38.6 5.1 %collective-permute-start = (bf16[1,23,1,146]{3,1,2,0:T(8,128)(2,1)S(1)}, bf16[1,23,1,146]{3,1,2,0:T(8,128)(2,1)S(1)}, u32[]{:S(2)}, u32[]{:S(2)}) collective-permute-start(bf16[1,23,1,146]{3,1,2,0:T(8,128)(2,1)S(1)} %bitcast.101), channel_id=1, source_target_pairs={{0,2},{2,0},{4,6},{6,4},{8,10},{10,8},{12,14},{14,12},{16,18},{18,... | collective-permute-start | bytes 20156 | tf_op jit(solution)/shard_map/ppermute | solution.py:59
  39.2 7.2 %collective-permute-start.1 = (bf16[1,23,1,146]{3,1,2,0:T(8,128)(2,1)S(1)}, bf16[1,23,1,146]{3,1,2,0:T(8,128)(2,1)S(1)}, u32[]{:S(2)}, u32[]{:S(2)}) collective-permute-start(bf16[1,23,1,146]{3,1,2,0:T(8,128)(2,1)S(1)} %bitcast.100), channel_id=1, source_target_pairs={{0,4},{2,6},{4,0},{6,2},{8,12},{10,14},{12,8},{14,10},{16,20},{18,... | collective-permute-start | bytes 20156 | tf_op jit(solution)/shard_map/ppermute | solution.py:59
  41.7 4.8 %collective-permute-start.2 = (bf16[1,23,1,146]{3,1,2,0:T(8,128)(2,1)S(1)}, bf16[1,23,1,146]{3,1,2,0:T(8,128)(2,1)S(1)}, u32[]{:S(2)}, u32[]{:S(2)}) collective-permute-start(bf16[1,23,1,146]{3,1,2,0:T(8,128)(2,1)S(1)} %bitcast.99), channel_id=1, source_target_pairs={{0,6},{2,4},{4,2},{6,0},{8,14},{10,12},{12,10},{14,8},{16,22},{18,... | collective-permute-start | bytes 20156 | tf_op jit(solution)/shard_map/ppermute | solution.py:59
  41.9 7.3 %collective-permute-start.3 = (bf16[1,23,1,146]{3,1,2,0:T(8,128)(2,1)S(1)}, bf16[1,23,1,146]{3,1,2,0:T(8,128)(2,1)S(1)}, u32[]{:S(2)}, u32[]{:S(2)}) collective-permute-start(bf16[1,23,1,146]{3,1,2,0:T(8,128)(2,1)S(1)} %bitcast.98), channel_id=1, source_target_pairs={{0,8},{2,10},{4,12},{6,14},{8,0},{10,2},{12,4},{14,6},{16,24},{18,... | collective-permute-start | bytes 20156 | tf_op jit(solution)/shard_map/ppermute | solution.py:59
  43.6 5.6 %collective-permute-start.4 = (bf16[1,23,1,146]{3,1,2,0:T(8,128)(2,1)S(1)}, bf16[1,23,1,146]{3,1,2,0:T(8,128)(2,1)S(1)}, u32[]{:S(2)}, u32[]{:S(2)}) collective-permute-start(bf16[1,23,1,146]{3,1,2,0:T(8,128)(2,1)S(1)} %bitcast.97), channel_id=1, source_target_pairs={{0,10},{2,8},{4,14},{6,12},{8,2},{10,0},{12,6},{14,4},{16,26},{18,... | collective-permute-start | bytes 20156 | tf_op jit(solution)/shard_map/ppermute | solution.py:59
  43.7 18.3 %collective-permute-start.5 = (bf16[1,23,1,146]{3,1,2,0:T(8,128)(2,1)S(1)}, bf16[1,23,1,146]{3,1,2,0:T(8,128)(2,1)S(1)}, u32[]{:S(2)}, u32[]{:S(2)}) collective-permute-start(bf16[1,23,1,146]{3,1,2,0:T(8,128)(2,1)S(1)} %bitcast.96), channel_id=1, source_target_pairs={{0,12},{2,14},{4,8},{6,10},{8,4},{10,6},{12,0},{14,2},{16,28},{18,... | collective-permute-start | bytes 20156 | tf_op jit(solution)/shard_map/ppermute | solution.py:59
  46.4 15.7 %collective-permute-start.6 = (bf16[1,23,1,146]{3,1,2,0:T(8,128)(2,1)S(1)}, bf16[1,23,1,146]{3,1,2,0:T(8,128)(2,1)S(1)}, u32[]{:S(2)}, u32[]{:S(2)}) collective-permute-start(bf16[1,23,1,146]{3,1,2,0:T(8,128)(2,1)S(1)} %bitcast.95), channel_id=1, source_target_pairs={{0,14},{2,12},{4,10},{6,8},{8,6},{10,4},{12,2},{14,0},{16,30},{18,... | collective-permute-start | bytes 20156 | tf_op jit(solution)/shard_map/ppermute | solution.py:59
  46.5 19.2 %collective-permute-start.7 = (bf16[1,23,1,146]{3,1,2,0:T(8,128)(2,1)S(1)}, bf16[1,23,1,146]{3,1,2,0:T(8,128)(2,1)S(1)}, u32[]{:S(2)}, u32[]{:S(2)}) collective-permute-start(bf16[1,23,1,146]{3,1,2,0:T(8,128)(2,1)S(1)} %bitcast.94), channel_id=1, source_target_pairs={{0,16},{2,18},{4,20},{6,22},{8,24},{10,26},{12,28},{14,30},{16,0},... | collective-permute-start | bytes 20156 | tf_op jit(solution)/shard_map/ppermute | solution.py:59
  49.2 16.6 %collective-permute-start.8 = (bf16[1,23,1,146]{3,1,2,0:T(8,128)(2,1)S(1)}, bf16[1,23,1,146]{3,1,2,0:T(8,128)(2,1)S(1)}, u32[]{:S(2)}, u32[]{:S(2)}) collective-permute-start(bf16[1,23,1,146]{3,1,2,0:T(8,128)(2,1)S(1)} %bitcast.93), channel_id=1, source_target_pairs={{0,18},{2,16},{4,22},{6,20},{8,26},{10,24},{12,30},{14,28},{16,2},... | collective-permute-start | bytes 20156 | tf_op jit(solution)/shard_map/ppermute | solution.py:59
  49.2 21.0 %collective-permute-start.9 = (bf16[1,23,1,146]{3,1,2,0:T(8,128)(2,1)S(1)}, bf16[1,23,1,146]{3,1,2,0:T(8,128)(2,1)S(1)}, u32[]{:S(2)}, u32[]{:S(2)}) collective-permute-start(bf16[1,23,1,146]{3,1,2,0:T(8,128)(2,1)S(1)} %bitcast.92), channel_id=1, source_target_pairs={{0,20},{2,22},{4,16},{6,18},{8,28},{10,30},{12,24},{14,26},{16,4},... | collective-permute-start | bytes 20156 | tf_op jit(solution)/shard_map/ppermute | solution.py:59
  52.7 17.6 %copy-start.2 = (s32[368]{0:T(512)S(1)}, s32[368]{0:T(512)}, u32[]{:S(2)}) copy-start(s32[368]{0:T(512)} %param.10) | copy-start | bytes 4420
  62.0 25.3 %collective-permute-start.10 = (bf16[1,23,1,146]{3,1,2,0:T(8,128)(2,1)S(1)}, bf16[1,23,1,146]{3,1,2,0:T(8,128)(2,1)S(1)}, u32[]{:S(2)}, u32[]{:S(2)}) collective-permute-start(bf16[1,23,1,146]{3,1,2,0:T(8,128)(2,1)S(1)} %bitcast.91), channel_id=1, source_target_pairs={{0,22},{2,20},{4,18},{6,16},{8,30},{10,28},{12,26},{14,24},{16,6},... | collective-permute-start | bytes 20156 | tf_op jit(solution)/shard_map/ppermute | solution.py:59
  62.1 25.8 %collective-permute-start.11 = (bf16[1,23,1,146]{3,1,2,0:T(8,128)(2,1)S(1)}, bf16[1,23,1,146]{3,1,2,0:T(8,128)(2,1)S(1)}, u32[]{:S(2)}, u32[]{:S(2)}) collective-permute-start(bf16[1,23,1,146]{3,1,2,0:T(8,128)(2,1)S(1)} %bitcast.90), channel_id=1, source_target_pairs={{0,24},{2,26},{4,28},{6,30},{8,16},{10,18},{12,20},{14,22},{16,8},... | collective-permute-start | bytes 20156 | tf_op jit(solution)/shard_map/ppermute | solution.py:59
  65.7 22.8 %collective-permute-start.12 = (bf16[1,23,1,146]{3,1,2,0:T(8,128)(2,1)S(1)}, bf16[1,23,1,146]{3,1,2,0:T(8,128)(2,1)S(1)}, u32[]{:S(2)}, u32[]{:S(2)}) collective-permute-start(bf16[1,23,1,146]{3,1,2,0:T(8,128)(2,1)S(1)} %bitcast.89), channel_id=1, source_target_pairs={{0,26},{2,24},{4,30},{6,28},{8,18},{10,16},{12,22},{14,20},{16,10}... | collective-permute-start | bytes 20156 | tf_op jit(solution)/shard_map/ppermute | solution.py:59
  65.8 23.3 %collective-permute-start.13 = (bf16[1,23,1,146]{3,1,2,0:T(8,128)(2,1)S(1)}, bf16[1,23,1,146]{3,1,2,0:T(8,128)(2,1)S(1)}, u32[]{:S(2)}, u32[]{:S(2)}) collective-permute-start(bf16[1,23,1,146]{3,1,2,0:T(8,128)(2,1)S(1)} %bitcast.88), channel_id=1, source_target_pairs={{0,28},{2,30},{4,24},{6,26},{8,20},{10,22},{12,16},{14,18},{16,12}... | collective-permute-start | bytes 20156 | tf_op jit(solution)/shard_map/ppermute | solution.py:59
  70.2 19.5 %collective-permute-start.14 = (bf16[1,23,1,146]{3,1,2,0:T(8,128)(2,1)S(1)}, bf16[1,23,1,146]{3,1,2,0:T(8,128)(2,1)S(1)}, u32[]{:S(2)}, u32[]{:S(2)}) collective-permute-start(bf16[1,23,1,146]{3,1,2,0:T(8,128)(2,1)S(1)} %bitcast.87), channel_id=1, source_target_pairs={{0,30},{2,28},{4,26},{6,24},{8,22},{10,20},{12,18},{14,16},{16,14}... | collective-permute-start | bytes 20156 | tf_op jit(solution)/shard_map/ppermute | solution.py:59
Sparse Core Ops, SparseCore 0:
  62.0 51.9 reduce-scatter.3
